TPU v7x, 256 devices: a whole 4x4x8 slice. The times are simulated.
256 devices in a mesh: row: 16 (over y, x), col: 16 (over z, core).
Axes of the slice: x: 4, y: 4, z: 8, core: 2. Of those that a mesh axis runs over, the one named last changes fastest.
Arguments:
- features: bfloat16 [512, 512, 128], P('col')
- diag_inverse: bfloat16 [512, 128, 128], P('col')
- precision_tiles: float32 [16, 16, 32, 128, 128], P('row', 'col'), may hold values from -3 to 3
- inverse_tiles: float32 [16, 16, 32, 128, 128], P('row', 'col'), may hold values from -0.3125 to 0.3125
- slot_rows: int32 [16, 16, 32], replicated, may hold values from 0 to 511, as said below
- slot_columns: int32 [16, 16, 32], replicated, may hold values from 0 to 1, as said below
- owned_columns: int32 [16, 16, 2], replicated, may hold values from 0 to 511, as said below
- live_counts: int32 [16, 16], replicated, may hold values from 1 to 32, as said below
Outputs:
- direction: float32 [16, 16, 32, 128, 128], P('row', 'col')
Inputs may be any that keep to these rules, and one draw needn't show every extreme that they name: `slot_rows`: slot k of every owner names a block-row held by index k // 2 of col, that is one of feature blocks 32 * (k // 2) to 32 * (k // 2) + 31; no pair of block-row and block-column is named by two slots of the whole grid. `slot_columns`: some owner uses every entry of its list. `owned_columns`: an owner's 2 block-columns are distinct and lie among the feature blocks of its own index of col. The live slots of an owner are slots 0 to live_counts - 1; some owner has all 32 slots live.
All inputs are finite; a program needn't handle non-finite values.
Results may differ from a plain program's by a relative error of at most 0.0003.
Values may be sent and summed in bfloat16 or wider, within the bound.
No kernel may reach another device: no remote copies, remote signals or barrier semaphores. Data moves between devices by JAX's collectives and lax.ppermute only.
A program may use at most 128 MiB of HBM per device.

v0:
```python
import jax
import jax.numpy as jnp
from jax import lax
from jax.sharding import PartitionSpec as P

SWEEPS = 4
step_size = 0.3
penalty = 0.6
highest = lax.Precision.HIGHEST


def soft_update(precision_tile, direction, residual):
    shifted = precision_tile + direction - step_size * residual
    return (
        jnp.sign(shifted) * jnp.maximum(jnp.abs(shifted) - step_size * penalty, 0.0)
        - precision_tile
    )


def body(
    features,
    diag_inverse,
    precision_tiles,
    inverse_tiles,
    slot_rows,
    slot_columns,
    owned_columns,
    live_counts,
):
    col_count = lax.axis_size("col")
    row_index = lax.axis_index("row")
    col_index = lax.axis_index("col")
    block_count = features.shape[0]
    sample_count = features.shape[1]
    block_size = features.shape[2]
    slot_count = precision_tiles.shape[2]
    per_source = slot_count // col_count
    row_table = slot_rows[row_index]
    wanted = jnp.take(row_table.reshape(col_count, col_count, per_source), col_index, axis=1)
    local_rows = (wanted - col_index * block_count).reshape(-1)
    send_tiles = jnp.take(features, local_rows, axis=0).reshape(
        col_count, per_source, sample_count, block_size
    )
    send_diag = jnp.take(diag_inverse, local_rows, axis=0).reshape(
        col_count, per_source, block_size, block_size
    )
    row_tiles, row_diag = (
        lax.all_to_all(send_tiles, "col", split_axis=0, concat_axis=0, tiled=True),
        lax.all_to_all(send_diag, "col", split_axis=0, concat_axis=0, tiled=True),
    )
    row_tiles = row_tiles.reshape(slot_count, sample_count, block_size)
    row_diag = row_diag.reshape(slot_count, block_size, block_size).astype(jnp.float32)
    my_lists = slot_columns[row_index, col_index]
    my_owned = owned_columns[row_index, col_index]
    column_ids = jnp.take(my_owned, my_lists)
    local_cols = column_ids - col_index * block_count
    live_mask = (jnp.arange(slot_count) < live_counts[row_index, col_index]).astype(jnp.float32)
    col_tiles = jnp.take(features, local_cols, axis=0)
    covariance = (
        jnp.einsum("kna,knb->kab", row_tiles, col_tiles, preferred_element_type=jnp.float32)
        / sample_count
    )
    tiles_here = inverse_tiles[0, 0]
    theta_here = precision_tiles[0, 0]
    gradient = covariance - tiles_here
    col_diag = jnp.take(diag_inverse, local_cols, axis=0).astype(jnp.float32)
    direction = jnp.zeros_like(gradient)
    for sweep_index in range(SWEEPS):
        residual = gradient
        if sweep_index > 0:
            left_side = jnp.einsum("kab,kbc->kac", row_diag, direction, precision=highest)
            residual = residual + jnp.einsum("kac,kcd->kad", left_side, col_diag, precision=highest)
            products = (
                jnp.einsum("kba,kbc->kac", direction, tiles_here, precision=highest)
                * live_mask[:, None, None]
            )
            onehot = (local_cols[:, None] == jnp.arange(block_count)[None, :]).astype(jnp.float32)
            dense_sums = jnp.einsum("kf,kab->fab", onehot, products, precision=highest)
            summed = lax.psum(dense_sums, "row")
            residual = residual + jnp.einsum(
                "kab,kbc->kac",
                tiles_here,
                jnp.einsum("kf,fab->kab", onehot, summed, precision=highest),
                precision=highest,
            )
        direction = soft_update(theta_here, direction, residual)
    return (direction * live_mask[:, None, None]).reshape(precision_tiles.shape)


def solution(mesh):
    return jax.shard_map(
        body,
        mesh=mesh,
        in_specs=(
            P("col", None, None),
            P("col", None, None),
            P("row", "col", None, None, None),
            P("row", "col", None, None, None),
            P(),
            P(),
            P(),
            P(),
        ),
        out_specs=P("row", "col", None, None, None),
        check_vma=False,
    )
```

profile of v0, /device:TPU:1, one launch (start us, length us, event | category | flops | bytes accessed | tf_op | source)
XLA Modules:
  0.0 511.0 jit_solution(2454693895170861494)
XLA Ops:
  6.5 0.0 copy-start
  6.5 0.8 constant_dynamic-slice_fusion
  7.4 0.5 fusion.89
  7.9 0.7 constant_dynamic-slice_fusion.2
  8.6 0.1 copy.34
  8.7 0.1 copy.14
  8.8 0.1 sub.61
  8.9 2.0 compare_and_fusion
  10.9 5.2 %gather_fusion = bf16[32,512,128]{2,1,0:T(8,128)(2,1)} fusion(bf16[32,512,128]{2,1,0:T(8,128)(2,1)} %param.12, s32[1024]{0:T(1024)S(1)} %pad_clamp_fusion.1), kind=kCustom, calls=%fused_computation.clone | custom fusion | bytes 8388736 | tf_op jit(solution)/shard_map/jit(_take)/gather | solution.py:41
  16.1 4.6 broadcast_select_fusion
  20.7 6.5 %copy.15 = bf16[16,2,512,128]{2,3,1,0:T(8,128)(2,1)} copy(bf16[16,2,512,128]{3,2,1,0:T(8,128)(2,1)} %bitcast.129) | data formatting | bytes 8388608 | tf_op jit(solution)/shard_map/reshape | solution.py:41
  27.2 10.0 %all-to-all-start = ((bf16[16,2,512,128]{2,3,1,0:T(8,128)(2,1)}), bf16[16,2,512,128]{2,3,1,0:T(8,128)(2,1)}, u32[]{:S(2)}, u32[]{:S(2)}) async-start(bf16[16,2,512,128]{2,3,1,0:T(8,128)(2,1)} %copy.15), calls=%async_computation | async-start | bytes 8388608 | tf_op jit(solution)/shard_map/all_to_all | solution.py:48
  37.1 1.3 dynamic_slice.15
  38.4 0.0 copy-done
  38.4 1.6 gather_fusion.2
  40.1 5.2 %gather_fusion.1 = bf16[32,512,128]{2,1,0:T(8,128)(2,1)} fusion(bf16[32,512,128]{2,1,0:T(8,128)(2,1)} %param.12, s32[1024]{0:T(1024)S(1)} %pad_clamp_fusion), kind=kCustom, calls=%fused_computation.2.clone | custom fusion | bytes 8388736 | tf_op jit(solution)/shard_map/jit(_take)/gather | solution.py:58
  45.3 0.6 compare_convert_fusion
  45.9 0.0 copy-start.2
  45.9 2.5 broadcast_select_fusion.2
  48.5 82.3 %all-to-all-done = bf16[16,2,512,128]{2,3,1,0:T(8,128)(2,1)} async-done(((bf16[16,2,512,128]{2,3,1,0:T(8,128)(2,1)}), bf16[16,2,512,128]{2,3,1,0:T(8,128)(2,1)}, u32[]{:S(2)}, u32[]{:S(2)}) %all-to-all-start) | async-done | bytes 4194336 | tf_op jit(solution)/shard_map/all_to_all | solution.py:48
  130.7 5.5 %all-to-all-start.1 = ((bf16[16,2,128,128]{3,2,1,0:T(8,128)(2,1)}), bf16[16,2,128,128]{3,2,1,0:T(8,128)(2,1)}, u32[]{:S(2)}, u32[]{:S(2)}) async-start(bf16[16,2,128,128]{3,2,1,0:T(8,128)(2,1)} %bitcast.130), calls=%async_computation.1 | async-start | bytes 2097152 | tf_op jit(solution)/shard_map/all_to_all | solution.py:49
  136.3 0.2 all-reduce.4.cloned.1.call-start
  136.5 0.0 copy-done.2
  136.5 0.0 copy-start.3
  136.5 4.9 bitcast_subtract_fusion
  141.4 0.0 copy-done.3
  141.4 0.0 copy-start.7
  141.5 4.5 fusion.39
  146.0 0.0 copy-done.7
  146.0 2.5 fusion.36
  148.5 2.5 copy.20
  151.0 0.0 all-reduce.4.cloned.1.call-update
  151.0 0.3 all-reduce.6.cloned.1.call-start
  151.3 1.7 gather_fusion.3
  153.0 11.3 %all-to-all-done.1 = bf16[16,2,128,128]{3,2,1,0:T(8,128)(2,1)} async-done(((bf16[16,2,128,128]{3,2,1,0:T(8,128)(2,1)}), bf16[16,2,128,128]{3,2,1,0:T(8,128)(2,1)}, u32[]{:S(2)}, u32[]{:S(2)}) %all-to-all-start.1) | async-done | bytes 1048608 | tf_op jit(solution)/shard_map/all_to_all | solution.py:49
  164.3 4.8 fusion.62
  169.1 0.0 copy-done.13
  169.1 2.6 fusion.87
  171.7 79.8 %all-reduce.4.cloned.1.call-done = f32[32,128,128]{2,1,0:T(8,128)} async-done(((f32[32,128,128]{2,1,0:T(8,128)}), f32[32,128,128]{2,1,0:T(8,128)}) %all-reduce.4.cloned.1.call-update) | async-done | bytes 2097168 | tf_op jit(solution)/shard_map/psum | solution.py:79
  251.5 4.1 fusion.34
  255.6 0.0 copy-done.4
  255.6 0.0 copy-done.8
  255.6 6.9 %bitcast_subtract_fusion.3 = f32[32,128,128]{2,1,0:T(8,128)S(1)} fusion(f32[1,1,32,128,128]{4,3,2,1,0:T(8,128)S(1)} %copy-done.4, f32[32,128,128]{2,1,0:T(8,128)S(1)} %copy-done.8, f32[32,128,128]{2,1,0:T(8,128)} %fusion.87, f32[1,1,32,128,128]{4,3,2,1,0:T(8,128)S(1)} %copy-done.2, f32[32,128,128]{2,0,1:T(8,128)S(1)} %fusion.34), kind=kOutput, calls=%fused_computation.34 | convolution fusion | flops 815267840 | bytes 12582912 | tf_op jit(solution)/shard_map/kab,kbc->kac/dot_general | solution.py:80
  262.5 4.3 fusion.42
  266.8 2.5 fusion.31
  269.3 2.6 copy.25
  271.9 0.0 all-reduce.6.cloned.1.call-update
  271.9 0.0 all-reduce.8.cloned.1.call-start
  272.0 3.2 fusion.90
  275.1 2.5 fusion.86
  277.7 94.3 %all-reduce.6.cloned.1.call-done = f32[32,128,128]{2,1,0:T(8,128)} async-done(((f32[32,128,128]{2,1,0:T(8,128)}), f32[32,128,128]{2,1,0:T(8,128)}) %all-reduce.6.cloned.1.call-update) | async-done | bytes 2097168 | tf_op jit(solution)/shard_map/psum | solution.py:79
  371.9 4.1 fusion.29
  376.0 6.9 %bitcast_subtract_fusion.2 = f32[32,128,128]{2,1,0:T(8,128)S(1)} fusion(f32[1,1,32,128,128]{4,3,2,1,0:T(8,128)S(1)} %copy-done.5, f32[32,128,128]{2,1,0:T(8,128)} %copy-done.12, f32[32,128,128]{2,1,0:T(8,128)S(1)} %copy-done.9, f32[32,128,128]{2,1,0:T(8,128)} %fusion.86, f32[1,1,32,128,128]{4,3,2,1,0:T(8,128)S(1)} %copy-done.2, f32[32,128,128]{2,0,1:T(8,128)S(1)} %fusion.29), kind=kOutput, calls=%fused_computation.32 | convolution fusion | flops 811073536 | bytes 14680064 | tf_op jit(solution)/shard_map/kab,kbc->kac/dot_general | solution.py:80
  383.0 0.0 copy-start.11
  383.0 4.0 fusion.45
  387.0 2.5 fusion.26
  389.5 2.6 copy.30
  392.1 0.0 all-reduce.8.cloned.1.call-update
  392.1 3.2 fusion.91
  395.3 2.6 fusion.85
  397.8 94.2 %all-reduce.8.cloned.1.call-done = f32[32,128,128]{2,1,0:T(8,128)} async-done(((f32[32,128,128]{2,1,0:T(8,128)}), f32[32,128,128]{2,1,0:T(8,128)}) %all-reduce.8.cloned.1.call-update) | async-done | bytes 2097168 | tf_op jit(solution)/shard_map/psum | solution.py:79
  492.0 4.3 fusion.24
  496.4 0.0 copy-start.1
  496.4 7.9 %fusion.22 = f32[1,1,32,128,128]{4,3,2,1,0:T(8,128)} fusion(f32[1,1,32,128,128]{4,3,2,1,0:T(8,128)S(1)} %copy-done.6, f32[32,128,128]{2,1,0:T(8,128)} %copy-done.11, f32[32,128,128]{2,1,0:T(8,128)S(1)} %copy-done.10, f32[32,128,128]{2,1,0:T(8,128)} %fusion.85, f32[1,1,32,128,128]{4,3,2,1,0:T(8,128)S(1)} %copy-done.2, f32[32,128,128]{2,0,1:T(8,128)S(1)} %fusion.24, ...), kind=kOutput, calls=%fused_computation.39 | convolution fusion | flops 811597824 | bytes 14680192 | tf_op jit(solution)/shard_map/kab,kbc->kac/dot_general | solution.py:80
  (20 shorter events, 0.1 us)
Async XLA Ops:
  6.5 31.9 %copy-start = (bf16[32,128,128]{2,1,0:T(8,128)(2,1)S(1)}, bf16[32,128,128]{2,1,0:T(8,128)(2,1)}, u32[]{:S(2)}) copy-start(bf16[32,128,128]{2,1,0:T(8,128)(2,1)} %param.13) | copy-start | bytes 3145732
  27.2 103.6 %all-to-all-start = ((bf16[16,2,512,128]{2,3,1,0:T(8,128)(2,1)}), bf16[16,2,512,128]{2,3,1,0:T(8,128)(2,1)}, u32[]{:S(2)}, u32[]{:S(2)}) async-start(bf16[16,2,512,128]{2,3,1,0:T(8,128)(2,1)} %copy.15), calls=%async_computation | async-start | bytes 8388608 | tf_op jit(solution)/shard_map/all_to_all | solution.py:48
  45.9 90.6 %copy-start.2 = (f32[1,1,32,128,128]{4,3,2,1,0:T(8,128)S(1)}, f32[1,1,32,128,128]{4,3,2,1,0:T(8,128)}, u32[]{:S(2)}) copy-start(f32[1,1,32,128,128]{4,3,2,1,0:T(8,128)} %param.15) | copy-start | bytes 6291460
  130.7 33.6 %all-to-all-start.1 = ((bf16[16,2,128,128]{3,2,1,0:T(8,128)(2,1)}), bf16[16,2,128,128]{3,2,1,0:T(8,128)(2,1)}, u32[]{:S(2)}, u32[]{:S(2)}) async-start(bf16[16,2,128,128]{3,2,1,0:T(8,128)(2,1)} %bitcast.130), calls=%async_computation.1 | async-start | bytes 2097152 | tf_op jit(solution)/shard_map/all_to_all | solution.py:49
  136.3 115.2 %all-reduce.4.cloned.1.call-start = ((), (), s32[]{:S(2)}) async-start(), calls=%async_computation.2 | async-start | bytes 4194304 | tf_op jit(solution)/shard_map/psum | solution.py:79
  136.5 4.9 copy-start.3
  141.4 4.5 copy-start.7
  151.0 220.9 %all-reduce.6.cloned.1.call-start = ((), (), s32[]{:S(2)}) async-start(), calls=%async_computation.3 | async-start | bytes 4194304 | tf_op jit(solution)/shard_map/psum | solution.py:79
  164.3 4.8 copy-start.13
  251.5 4.1 copy-start.4
  251.5 4.1 copy-start.8
  262.5 4.3 copy-start.12
  271.9 220.1 %all-reduce.8.cloned.1.call-start = ((), (), s32[]{:S(2)}) async-start(), calls=%async_computation.4 | async-start | bytes 4194304 | tf_op jit(solution)/shard_map/psum | solution.py:79
  371.9 4.1 copy-start.5
  371.9 4.1 copy-start.9
  383.0 4.0 copy-start.11
  492.0 4.3 copy-start.6
  492.0 4.3 copy-start.10
  496.4 7.9 %copy-start.1 = (bf16[32,128,128]{2,1,0:T(8,128)(2,1)S(1)}, bf16[32,128,128]{2,1,0:T(8,128)(2,1)}, u32[]{:S(2)}) copy-start(bf16[32,128,128]{2,1,0:T(8,128)(2,1)} %param.13) | copy-start | bytes 3145732
Sparse Core Ops, SparseCore 0:
  151.2 100.2 all-reduce.3
  272.0 99.8 all-reduce.5
  392.2 99.7 all-reduce.7
where the time goes:
time: 514 us; the launch traced here: 511 us
  waiting for transfers between devices  362 us (70%)
  matrix products  78.1 us (15%)
  local copies, waits for them, and re-layouts  31.6 us (6%)
  starting transfers between devices  16 us (3%)
  between operations  13.6 us (3%)
  other arithmetic  9.75 us (2%)
    psum x3, waiting for transfers between devices, body(): summed = lax.psum(dense_sums, 'row')  268 us
    all_to_all x1, waiting for transfers between devices, body(): lax.all_to_all(send_tiles, 'col', split_axis=0, concat_axis=0, tiled=True)  82.3 us
    dot_general x3, matrix products, body(): jnp.einsum('kab,kbc->kac', tiles_here, jnp.einsum('kf,fab->kab', onehot,...  21.7 us
    dot_general x3, matrix products, body(): jnp.einsum('kba,kbc->kac', direction, tiles_here, precision=highest)  12.8 us
    dot_general x3, matrix products, body(): jnp.einsum('kf,fab->kab', onehot, summed, precision=highest)  12.4 us
    all_to_all x1, waiting for transfers between devices, body(): lax.all_to_all(send_diag, 'col', split_axis=0, concat_axis=0, tiled=True)  11.3 us
    dot_general x3, matrix products, body(): jnp.einsum('kab,kbc->kac', row_diag, direction, precision=highest)  11.1 us
  transfers between devices with their start and end apart: 5, of which 5 were waited for; matrix products, arithmetic and copies ran while one was open for 9% of the time, Pallas kernels for 0%

commit v1 on v0

--- a/solution.py
+++ b/solution.py
@@ -2,6 +2,7 @@
 import jax.numpy as jnp
 from jax import lax
 from jax.sharding import PartitionSpec as P
+from jax.lax import axis_size, ppermute
 
 SWEEPS = 4
 step_size = 0.3
@@ -76,7 +77,13 @@
             )
             onehot = (local_cols[:, None] == jnp.arange(block_count)[None, :]).astype(jnp.float32)
             dense_sums = jnp.einsum("kf,kab->fab", onehot, products, precision=highest)
-            summed = lax.psum(dense_sums, "row")
+            how_many = axis_size("row")
+            summed = dense_sums
+            for i0 in [
+                [(b, b ^ q) for b in range(how_many)] for q in (1, 2, 4, 8, 16) if q < how_many
+            ]:
+                taken_in = ppermute(summed, "row", i0)
+                summed = summed + taken_in
             residual = residual + jnp.einsum(
                 "kab,kbc->kac",
                 tiles_here,

time: 514 us -> 736 us (1.43)
  the two profiles are of different devices: /device:TPU:1 before, /device:TPU:62 now
where the time goes in v1:
time: 736 us; the launch traced here: 727 us
  waiting for transfers between devices  576 us (78%)
  matrix products  60.5 us (8%)
  starting transfers between devices  47.4 us (6%)
  local copies, waits for them, and re-layouts  24 us (3%)
  other arithmetic  18.7 us (3%)
    ppermute x12, waiting for transfers between devices, body(): taken_in = ppermute(summed, 'row', i0)  491 us
    all_to_all x1, waiting for transfers between devices, body(): lax.all_to_all(send_tiles, 'col', split_axis=0, concat_axis=0, tiled=True)  85.1 us
    ppermute x12, starting transfers between devices, body(): taken_in = ppermute(summed, 'row', i0)  32.7 us
    dot_general x3, matrix products, body(): jnp.einsum('kab,kbc->kac', tiles_here, jnp.einsum('kf,fab->kab', onehot,...  15.8 us
  transfers between devices with their start and end apart: 14, of which 13 were waited for; matrix products, arithmetic and copies ran while one was open for 4% of the time, Pallas kernels for 0%

profile of v1, /device:TPU:62, one launch (start us, length us, event | category | flops | bytes accessed | tf_op | source)
XLA Modules:
  0.0 727.0 jit_solution(5110879044679770878)
XLA Ops:
  0.0 0.8 constant_dynamic-slice_fusion
  0.8 0.5 fusion.89
  1.4 0.7 constant_dynamic-slice_fusion.2
  2.3 1.9 compare_and_fusion
  4.3 5.3 gather_fusion
  9.6 4.7 broadcast_select_fusion
  14.3 6.4 copy.18
  20.6 8.6 %all-to-all-start = ((bf16[16,2,512,128]{2,3,1,0:T(8,128)(2,1)}), bf16[16,2,512,128]{2,3,1,0:T(8,128)(2,1)}, u32[]{:S(2)}, u32[]{:S(2)}) async-start(bf16[16,2,512,128]{2,3,1,0:T(8,128)(2,1)} %copy.18), calls=%async_computation | async-start | bytes 8388608 | tf_op jit(solution)/shard_map/all_to_all | solution.py:49
  29.3 5.4 gather_fusion.1
  34.7 1.3 dynamic_slice.15
  35.9 0.6 compare_convert_fusion
  36.6 85.1 %all-to-all-done = bf16[16,2,512,128]{2,3,1,0:T(8,128)(2,1)} async-done(((bf16[16,2,512,128]{2,3,1,0:T(8,128)(2,1)}), bf16[16,2,512,128]{2,3,1,0:T(8,128)(2,1)}, u32[]{:S(2)}, u32[]{:S(2)}) %all-to-all-start) | async-done | bytes 4194336 | tf_op jit(solution)/shard_map/all_to_all | solution.py:49
  121.7 4.9 bitcast_subtract_fusion
  126.7 4.5 fusion.39
  131.2 2.5 fusion.30
  133.7 0.9 collective-permute-start
  134.6 47.0 %collective-permute-done = f32[32,128,128]{2,0,1:T(8,128)S(1)} collective-permute-done((f32[32,128,128]{2,0,1:T(8,128)S(1)}, f32[32,128,128]{2,0,1:T(8,128)S(1)}, u32[]{:S(2)}, u32[]{:S(2)}) %collective-permute-start) | collective-permute-done | bytes 2097184 | tf_op jit(solution)/shard_map/ppermute | solution.py:85
  181.6 0.5 add.124
  182.1 1.7 collective-permute-start.1
  183.8 47.1 %collective-permute-done.1 = f32[32,128,128]{2,0,1:T(8,128)S(1)} collective-permute-done((f32[32,128,128]{2,0,1:T(8,128)S(1)}, f32[32,128,128]{2,0,1:T(8,128)S(1)}, u32[]{:S(2)}, u32[]{:S(2)}) %collective-permute-start.1) | collective-permute-done | bytes 2097184 | tf_op jit(solution)/shard_map/ppermute | solution.py:85
  230.9 1.8 add.125
  232.7 0.7 collective-permute-start.2
  233.4 1.6 gather_fusion.2
  235.0 2.3 broadcast_select_fusion.2
  237.4 6.1 all-to-all-start.1
  243.5 35.6 %collective-permute-done.2 = f32[32,128,128]{2,0,1:T(8,128)} collective-permute-done((f32[32,128,128]{2,0,1:T(8,128)}, f32[32,128,128]{2,0,1:T(8,128)}, u32[]{:S(2)}, u32[]{:S(2)}) %collective-permute-start.2) | collective-permute-done | bytes 2097184 | tf_op jit(solution)/shard_map/ppermute | solution.py:85
  279.1 4.0 add.126
  283.1 1.5 collective-permute-start.3
  284.5 1.7 gather_fusion.3
  286.2 4.8 fusion.62
  291.0 1.2 fusion.87
  292.2 38.1 %collective-permute-done.3 = f32[32,128,128]{2,0,1:T(8,128)} collective-permute-done((f32[32,128,128]{2,0,1:T(8,128)}, f32[32,128,128]{2,0,1:T(8,128)}, u32[]{:S(2)}, u32[]{:S(2)}) %collective-permute-start.3) | collective-permute-done | bytes 2097184 | tf_op jit(solution)/shard_map/ppermute | solution.py:85
  330.3 3.4 fusion.37
  333.7 5.4 bitcast_subtract_fusion.3
  339.1 4.4 fusion.42
  343.6 2.5 fusion.28
  346.0 0.9 collective-permute-start.4
  346.9 45.1 %collective-permute-done.4 = f32[32,128,128]{2,0,1:T(8,128)S(1)} collective-permute-done((f32[32,128,128]{2,0,1:T(8,128)S(1)}, f32[32,128,128]{2,0,1:T(8,128)S(1)}, u32[]{:S(2)}, u32[]{:S(2)}) %collective-permute-start.4) | collective-permute-done | bytes 2097184 | tf_op jit(solution)/shard_map/ppermute | solution.py:85
  392.1 0.5 add.131
  392.6 43.1 %collective-permute-done.5 = f32[32,128,128]{2,0,1:T(8,128)S(1)} collective-permute-done((f32[32,128,128]{2,0,1:T(8,128)S(1)}, f32[32,128,128]{2,0,1:T(8,128)S(1)}, u32[]{:S(2)}, u32[]{:S(2)}) %collective-permute-start.5) | collective-permute-done | bytes 2097184 | tf_op jit(solution)/shard_map/ppermute | solution.py:85
  435.8 0.5 add.132
  436.3 0.8 collective-permute-start.6
  437.1 45.1 %collective-permute-done.6 = f32[32,128,128]{2,0,1:T(8,128)S(1)} collective-permute-done((f32[32,128,128]{2,0,1:T(8,128)S(1)}, f32[32,128,128]{2,0,1:T(8,128)S(1)}, u32[]{:S(2)}, u32[]{:S(2)}) %collective-permute-start.6) | collective-permute-done | bytes 2097184 | tf_op jit(solution)/shard_map/ppermute | solution.py:85
  482.9 2.5 fusion.90
  485.4 1.2 fusion.86
  486.6 35.1 %collective-permute-done.7 = f32[32,128,128]{2,0,1:T(8,128)S(1)} collective-permute-done((f32[32,128,128]{2,0,1:T(8,128)S(1)}, f32[32,128,128]{2,0,1:T(8,128)S(1)}, u32[]{:S(2)}, u32[]{:S(2)}) %collective-permute-start.7) | collective-permute-done | bytes 2097184 | tf_op jit(solution)/shard_map/ppermute | solution.py:85
  521.7 1.2 fusion.35
  523.0 4.5 bitcast_subtract_fusion.2
  527.5 4.0 fusion.45
  531.5 2.7 fusion.26
  534.1 2.4 collective-permute-start.8
  536.5 37.4 %collective-permute-done.8 = f32[32,128,128]{2,0,1:T(8,128)S(1)} collective-permute-done((f32[32,128,128]{2,0,1:T(8,128)S(1)}, f32[32,128,128]{2,0,1:T(8,128)S(1)}, u32[]{:S(2)}, u32[]{:S(2)}) %collective-permute-start.8) | collective-permute-done | bytes 2097184 | tf_op jit(solution)/shard_map/ppermute | solution.py:85
  573.9 0.5 add.138
  574.4 12.2 %collective-permute-start.9 = (f32[32,128,128]{2,0,1:T(8,128)S(1)}, f32[32,128,128]{2,0,1:T(8,128)S(1)}, u32[]{:S(2)}, u32[]{:S(2)}) collective-permute-start(f32[32,128,128]{2,0,1:T(8,128)S(1)} %add.138), channel_id=1, source_target_pairs={{0,32},{16,48},{32,0},{48,16},{64,96},{80,112},{96,64},{112,80},{1... | collective-permute-start | bytes 6291464 | tf_op jit(solution)/shard_map/ppermute | solution.py:85
  586.7 38.9 %collective-permute-done.9 = f32[32,128,128]{2,0,1:T(8,128)S(1)} collective-permute-done((f32[32,128,128]{2,0,1:T(8,128)S(1)}, f32[32,128,128]{2,0,1:T(8,128)S(1)}, u32[]{:S(2)}, u32[]{:S(2)}) %collective-permute-start.9) | collective-permute-done | bytes 2097184 | tf_op jit(solution)/shard_map/ppermute | solution.py:85
  626.0 2.5 collective-permute-start.10
  628.5 39.9 %collective-permute-done.10 = f32[32,128,128]{2,0,1:T(8,128)S(1)} collective-permute-done((f32[32,128,128]{2,0,1:T(8,128)S(1)}, f32[32,128,128]{2,0,1:T(8,128)S(1)}, u32[]{:S(2)}, u32[]{:S(2)}) %collective-permute-start.10) | collective-permute-done | bytes 2097184 | tf_op jit(solution)/shard_map/ppermute | solution.py:85
  668.4 0.5 add.140
  668.9 8.7 %collective-permute-start.11 = (f32[32,128,128]{2,0,1:T(8,128)S(1)}, f32[32,128,128]{2,0,1:T(8,128)S(1)}, u32[]{:S(2)}, u32[]{:S(2)}) collective-permute-start(f32[32,128,128]{2,0,1:T(8,128)S(1)} %add.140), channel_id=1, source_target_pairs={{0,128},{16,144},{32,160},{48,176},{64,192},{80,208},{96,224},{112... | collective-permute-start | bytes 6291464 | tf_op jit(solution)/shard_map/ppermute | solution.py:85
  677.6 2.5 fusion.91
  680.1 1.2 fusion.85
  681.3 38.1 %collective-permute-done.11 = f32[32,128,128]{2,0,1:T(8,128)S(1)} collective-permute-done((f32[32,128,128]{2,0,1:T(8,128)S(1)}, f32[32,128,128]{2,0,1:T(8,128)S(1)}, u32[]{:S(2)}, u32[]{:S(2)}) %collective-permute-start.11) | collective-permute-done | bytes 2097184 | tf_op jit(solution)/shard_map/ppermute | solution.py:85
  719.4 1.2 fusion.33
  720.6 6.0 fusion.22
  (29 shorter events, 1.6 us)
Async XLA Ops:
  0.0 233.4 %copy-start = (bf16[32,128,128]{2,1,0:T(8,128)(2,1)S(1)}, bf16[32,128,128]{2,1,0:T(8,128)(2,1)}, u32[]{:S(2)}) copy-start(bf16[32,128,128]{2,1,0:T(8,128)(2,1)} %param.13) | copy-start | bytes 3145732
  20.6 101.1 %all-to-all-start = ((bf16[16,2,512,128]{2,3,1,0:T(8,128)(2,1)}), bf16[16,2,512,128]{2,3,1,0:T(8,128)(2,1)}, u32[]{:S(2)}, u32[]{:S(2)}) async-start(bf16[16,2,512,128]{2,3,1,0:T(8,128)(2,1)} %copy.18), calls=%async_computation | async-start | bytes 8388608 | tf_op jit(solution)/shard_map/all_to_all | solution.py:49
  29.2 92.5 %copy-start.2 = (f32[1,1,32,128,128]{4,3,2,1,0:T(8,128)S(1)}, f32[1,1,32,128,128]{4,3,2,1,0:T(8,128)}, u32[]{:S(2)}) copy-start(f32[1,1,32,128,128]{4,3,2,1,0:T(8,128)} %param.15) | copy-start | bytes 6291460
  121.7 4.9 copy-start.3
  126.7 4.5 copy-start.5
  133.7 47.9 %collective-permute-start = (f32[32,128,128]{2,0,1:T(8,128)S(1)}, f32[32,128,128]{2,0,1:T(8,128)S(1)}, u32[]{:S(2)}, u32[]{:S(2)}) collective-permute-start(f32[32,128,128]{2,0,1:T(8,128)S(1)} %fusion.30), channel_id=1, source_target_pairs={{0,16},{16,0},{32,48},{48,32},{64,80},{80,64},{96,112},{112,96},{1... | collective-permute-start | bytes 6291464 | tf_op jit(solution)/shard_map/ppermute | solution.py:85
  182.1 48.8 %collective-permute-start.1 = (f32[32,128,128]{2,0,1:T(8,128)S(1)}, f32[32,128,128]{2,0,1:T(8,128)S(1)}, u32[]{:S(2)}, u32[]{:S(2)}) collective-permute-start(f32[32,128,128]{2,0,1:T(8,128)S(1)} %add.124), channel_id=1, source_target_pairs={{0,32},{16,48},{32,0},{48,16},{64,96},{80,112},{96,64},{112,80},{1... | collective-permute-start | bytes 6291464 | tf_op jit(solution)/shard_map/ppermute | solution.py:85
  232.7 46.4 %collective-permute-start.2 = (f32[32,128,128]{2,0,1:T(8,128)}, f32[32,128,128]{2,0,1:T(8,128)}, u32[]{:S(2)}, u32[]{:S(2)}) collective-permute-start(f32[32,128,128]{2,0,1:T(8,128)} %add.125), channel_id=1, source_target_pairs={{0,64},{16,80},{32,96},{48,112},{64,0},{80,16},{96,32},{112,48},{1... | collective-permute-start | bytes 6291464 | tf_op jit(solution)/shard_map/ppermute | solution.py:85
  237.4 48.8 %all-to-all-start.1 = ((bf16[16,2,128,128]{3,2,1,0:T(8,128)(2,1)}), bf16[16,2,128,128]{3,2,1,0:T(8,128)(2,1)}, u32[]{:S(2)}, u32[]{:S(2)}) async-start(bf16[16,2,128,128]{3,2,1,0:T(8,128)(2,1)} %bitcast.130), calls=%async_computation.1 | async-start | bytes 2097152 | tf_op jit(solution)/shard_map/all_to_all | solution.py:50
  283.1 47.2 %collective-permute-start.3 = (f32[32,128,128]{2,0,1:T(8,128)}, f32[32,128,128]{2,0,1:T(8,128)}, u32[]{:S(2)}, u32[]{:S(2)}) collective-permute-start(f32[32,128,128]{2,0,1:T(8,128)} %add.126), channel_id=1, source_target_pairs={{0,128},{16,144},{32,160},{48,176},{64,192},{80,208},{96,224},{112... | collective-permute-start | bytes 6291464 | tf_op jit(solution)/shard_map/ppermute | solution.py:85
  286.2 4.8 copy-start.7
  292.2 41.5 %copy-start.4 = (f32[1,1,32,128,128]{4,3,2,1,0:T(8,128)S(1)}, f32[1,1,32,128,128]{4,3,2,1,0:T(8,128)}, u32[]{:S(2)}) copy-start(f32[1,1,32,128,128]{4,3,2,1,0:T(8,128)} %param.14) | copy-start | bytes 6291460
  292.2 41.5 %copy-start.6 = (f32[32,128,128]{2,1,0:T(8,128)S(1)}, f32[32,128,128]{2,1,0:T(8,128)}, u32[]{:S(2)}) copy-start(f32[32,128,128]{2,1,0:T(8,128)} %copy-done.5) | copy-start | bytes 6291460
  346.0 46.0 %collective-permute-start.4 = (f32[32,128,128]{2,0,1:T(8,128)S(1)}, f32[32,128,128]{2,0,1:T(8,128)S(1)}, u32[]{:S(2)}, u32[]{:S(2)}) collective-permute-start(f32[32,128,128]{2,0,1:T(8,128)S(1)} %fusion.28), channel_id=1, source_target_pairs={{0,16},{16,0},{32,48},{48,32},{64,80},{80,64},{96,112},{112,96},{1... | collective-permute-start | bytes 6291464 | tf_op jit(solution)/shard_map/ppermute | solution.py:85
  392.5 43.2 %collective-permute-start.5 = (f32[32,128,128]{2,0,1:T(8,128)S(1)}, f32[32,128,128]{2,0,1:T(8,128)S(1)}, u32[]{:S(2)}, u32[]{:S(2)}) collective-permute-start(f32[32,128,128]{2,0,1:T(8,128)S(1)} %add.131), channel_id=1, source_target_pairs={{0,32},{16,48},{32,0},{48,16},{64,96},{80,112},{96,64},{112,80},{1... | collective-permute-start | bytes 6291464 | tf_op jit(solution)/shard_map/ppermute | solution.py:85
  436.3 45.9 %collective-permute-start.6 = (f32[32,128,128]{2,0,1:T(8,128)S(1)}, f32[32,128,128]{2,0,1:T(8,128)S(1)}, u32[]{:S(2)}, u32[]{:S(2)}) collective-permute-start(f32[32,128,128]{2,0,1:T(8,128)S(1)} %add.132), channel_id=1, source_target_pairs={{0,64},{16,80},{32,96},{48,112},{64,0},{80,16},{96,32},{112,48},{1... | collective-permute-start | bytes 6291464 | tf_op jit(solution)/shard_map/ppermute | solution.py:85
  482.6 39.1 %collective-permute-start.7 = (f32[32,128,128]{2,0,1:T(8,128)S(1)}, f32[32,128,128]{2,0,1:T(8,128)S(1)}, u32[]{:S(2)}, u32[]{:S(2)}) collective-permute-start(f32[32,128,128]{2,0,1:T(8,128)S(1)} %add.133), channel_id=1, source_target_pairs={{0,128},{16,144},{32,160},{48,176},{64,192},{80,208},{96,224},{112... | collective-permute-start | bytes 6291464 | tf_op jit(solution)/shard_map/ppermute | solution.py:85
  534.1 39.8 %collective-permute-start.8 = (f32[32,128,128]{2,0,1:T(8,128)S(1)}, f32[32,128,128]{2,0,1:T(8,128)S(1)}, u32[]{:S(2)}, u32[]{:S(2)}) collective-permute-start(f32[32,128,128]{2,0,1:T(8,128)S(1)} %fusion.26), channel_id=1, source_target_pairs={{0,16},{16,0},{32,48},{48,32},{64,80},{80,64},{96,112},{112,96},{1... | collective-permute-start | bytes 6291464 | tf_op jit(solution)/shard_map/ppermute | solution.py:85
  574.4 51.1 %collective-permute-start.9 = (f32[32,128,128]{2,0,1:T(8,128)S(1)}, f32[32,128,128]{2,0,1:T(8,128)S(1)}, u32[]{:S(2)}, u32[]{:S(2)}) collective-permute-start(f32[32,128,128]{2,0,1:T(8,128)S(1)} %add.138), channel_id=1, source_target_pairs={{0,32},{16,48},{32,0},{48,16},{64,96},{80,112},{96,64},{112,80},{1... | collective-permute-start | bytes 6291464 | tf_op jit(solution)/shard_map/ppermute | solution.py:85
  626.0 42.4 %collective-permute-start.10 = (f32[32,128,128]{2,0,1:T(8,128)S(1)}, f32[32,128,128]{2,0,1:T(8,128)S(1)}, u32[]{:S(2)}, u32[]{:S(2)}) collective-permute-start(f32[32,128,128]{2,0,1:T(8,128)S(1)} %add.139), channel_id=1, source_target_pairs={{0,64},{16,80},{32,96},{48,112},{64,0},{80,16},{96,32},{112,48},{1... | collective-permute-start | bytes 6291464 | tf_op jit(solution)/shard_map/ppermute | solution.py:85
  668.9 50.5 %collective-permute-start.11 = (f32[32,128,128]{2,0,1:T(8,128)S(1)}, f32[32,128,128]{2,0,1:T(8,128)S(1)}, u32[]{:S(2)}, u32[]{:S(2)}) collective-permute-start(f32[32,128,128]{2,0,1:T(8,128)S(1)} %add.140), channel_id=1, source_target_pairs={{0,128},{16,144},{32,160},{48,176},{64,192},{80,208},{96,224},{112... | collective-permute-start | bytes 6291464 | tf_op jit(solution)/shard_map/ppermute | solution.py:85
  720.6 6.0 copy-start.1
